TPU v7x, 512 devices: a whole 4x8x8 slice. The times are simulated.
512 devices in a mesh: space: 16 (over x, y_lo, core), term: 32 (over z, y_hi).
Axes of the slice: x: 4, y: 8 (y_hi: 4, y_lo: 2; y = y_hi * 2 + y_lo), z: 8, core: 2. Of those that a mesh axis runs over, the one named last changes fastest.
Arguments:
- right_modes: float32 [512, 64, 256], P(('space', 'term')), may hold values from -0.015625 to 0.015625
- adjoint_modes: float32 [512, 64, 256], P(('space', 'term')), may hold values from -6 to 6
- conductivity_terms: float32 [512, 256, 256], P('space', 'term'), may hold values from -6 to 6
Outputs:
- reduced_blocks: float32 [256, 4096], P('term', 'space')
All inputs are finite; a program needn't handle non-finite values.
Results may differ from a plain program's by a relative error of at most 0.000098.
Values sent between devices are 32-bit elements; how exact they have to be, the bound alone decides.
A program may use at most 64 MiB of HBM per device.

v0:
```python
import jax
import jax.numpy as jnp
from jax import lax
from jax.sharding import PartitionSpec as P

GY = 32


def extended(block, sides, width):
    for axis, dim in sides:
        count = lax.axis_size(axis)
        forward = [(i, i + 1) for i in range(count - 1)]
        backward = [(target, source) for source, target in forward]
        low = lax.ppermute(
            lax.slice_in_dim(block, block.shape[dim] - width, None, axis=dim), axis, forward
        )
        high = lax.ppermute(lax.slice_in_dim(block, 0, width, axis=dim), axis, backward)
        block = jnp.concatenate([low, block, high], axis=dim)
    return block


def shifted_cells(values, offset):
    zeros = jnp.zeros(values.shape[:-1] + (abs(offset),), jnp.float32)
    if offset > 0:
        return jnp.concatenate([values[..., offset:], zeros], axis=-1)
    return jnp.concatenate([zeros, values[..., :offset]], axis=-1)


def apply_terms(field_pad, coeff_pad, row_len):
    width = field_pad.shape[-1]
    column = jnp.arange(width) % row_len
    keep_next = (column != row_len - 1).astype(jnp.float32)
    keep_prev = (column != 0).astype(jnp.float32)
    centre = field_pad[None, 1:-1]
    coeff = coeff_pad[:, 1:-1, None, :]
    pairs = [
        (field_pad[None, 2:], coeff_pad[:, 2:, None, :]),
        (field_pad[None, :-2], coeff_pad[:, :-2, None, :]),
        (shifted_cells(centre, row_len), shifted_cells(coeff, row_len)),
        (shifted_cells(centre, -row_len), shifted_cells(coeff, -row_len)),
        (shifted_cells(centre, 1) * keep_next, shifted_cells(coeff, 1) * keep_next),
        (shifted_cells(centre, -1) * keep_prev, shifted_cells(coeff, -1) * keep_prev),
    ]
    result = jnp.zeros(coeff.shape[:2] + centre.shape[2:], jnp.float32)
    for other_field, other_coeff in pairs:
        result = result + 0.5 * (coeff + other_coeff) * (centre - other_field)
    return result


def assemble(field_pad, coeff_pad, adjoint, per_turn):
    modes = field_pad.shape[1]
    terms = coeff_pad.shape[1]
    ordered = jnp.moveaxis(coeff_pad, 1, 0)
    ordered = ordered.reshape((terms // per_turn, per_turn) + ordered.shape[1:])

    def one_block(coeff_block):
        image = apply_terms(field_pad, coeff_block, GY)
        return jnp.einsum("zrp,gzsp->grs", adjoint, image, precision=lax.Precision.HIGHEST)

    blocks = lax.map(one_block, ordered)
    return blocks.reshape(terms, modes * modes)


def local(right_modes, adjoint_modes, conductivity_terms):
    modes = right_modes.shape[1]
    slab_right, slab_adjoint = (
        lax.all_gather(right_modes, "term", axis=0, tiled=True),
        lax.all_gather(adjoint_modes, "term", axis=0, tiled=True),
    )
    stacked = jnp.concatenate([slab_right, conductivity_terms], axis=1)
    padded = extended(stacked, (("space", 0),), 1)
    partial_value = assemble(padded[:, :modes], padded[:, modes:], slab_adjoint, 1)
    return lax.psum_scatter(partial_value, "space", scatter_dimension=1, tiled=True)


def solution(mesh):
    placed = (
        P(("space", "term"), None, None),
        P(("space", "term"), None, None),
        P("space", "term", None),
    )
    return jax.shard_map(
        local, mesh=mesh, in_specs=placed, out_specs=P("term", "space"), check_vma=False
    )
```

profile of v0, /device:TPU:16, one launch (start us, length us, event | category | flops | bytes accessed | tf_op | source)
XLA Modules:
  0.0 315.2 jit_solution(1327591688766280557)
XLA Ops:
  6.5 0.7 all-gather.3.cloned.1.call-update
  7.3 0.7 all-gather.5.cloned.1.call-update
  8.1 93.2 %all-gather.3.cloned.1.call-done = f32[32,64,256]{2,1,0:T(8,128)} async-done(((f32[1,64,256]{2,1,0:T(8,128)}), f32[32,64,256]{2,1,0:T(8,128)}) %all-gather.3.cloned.1.call-update) | async-done | bytes 2097168 | tf_op jit(solution)/shard_map/all_gather | solution.py:67
  101.3 1.7 constant_dynamic-update-slice_fusion.2
  103.1 1.4 copy-done.3
  104.5 1.3 collective-permute-start.1
  105.8 3.0 collective-permute-start
  108.9 0.9 collective-permute-done
  109.7 1.0 maximum_bitcast_fusion
  110.7 0.2 pad_maximum_fusion
  111.0 1.3 copy-done.5
  112.3 2.5 fusion.38
  114.8 72.1 %all-gather.5.cloned.1.call-done = f32[32,64,256]{2,1,0:T(8,128)} async-done(((f32[1,64,256]{2,1,0:T(8,128)}), f32[32,64,256]{2,1,0:T(8,128)}) %all-gather.5.cloned.1.call-update) | async-done | bytes 2097168 | tf_op jit(solution)/shard_map/all_gather | solution.py:68
  186.9 58.4 %while.12 = (s32[]{:T(128)}, f32[8,1,64,64]{3,2,0,1:T(8,128)S(1)}, f32[8,1,34,256]{3,0,2,1:T(8,128)S(1)}, f32[32,64,256]{2,1,0:T(8,128)}, f32[32,64,256]{2,1,0:T...) while((s32[]{:T(128)}, f32[8,1,64,64]{3,2,0,1:T(8,128)S(1)}, ...), condition=%wide.region_1.2_spmd, body=%wide.region_0.1_spmd.sunk | while | flops 411683328 | bytes 63018424 | solution.py:60
  187.1 0.8 fusion.56
  187.9 0.8 fusion.57
  189.1 0.4 copy-done
  189.5 0.6 copy-done.1
  190.1 0.6 copy-done.2
  190.8 3.3 %fusion.61 = f32[1,1,64,64]{2,3,1,0:T(8,128)S(1)} fusion(f32[32,64,256]{2,1,0:T(8,128)S(1)} %copy-done.2, f32[32,64,256]{2,1,0:T(8,128)S(1)} %copy-done, f32[32,64,256]{2,1,0:T(8,128)S(1)} %copy-done.1, f32[1,32,64,255]{3,2,1,0:T(8,128)S(1)} %get-tuple-element.192, f32[1,32,64,255]{3,2,1,0:T(8,128)S(1)} %get-tuple-element.193, ...), kind=kOutput, calls=%fused_computation.24.clone.1 | convolution fusion | flops 411566080 | bytes 16992256 | tf_op jit(solution)/shard_map/while/body/eval_jaxpr/zrp,gzsp->grs/dot_general | solution.py:58
  194.4 0.8 fusion.56
  195.2 0.8 fusion.57
  196.4 0.4 copy-done
  196.8 0.6 copy-done.1
  197.4 0.6 copy-done.2
  198.1 3.3 %fusion.61 = f32[1,1,64,64]{2,3,1,0:T(8,128)S(1)} fusion(f32[32,64,256]{2,1,0:T(8,128)S(1)} %copy-done.2, f32[32,64,256]{2,1,0:T(8,128)S(1)} %copy-done, f32[32,64,256]{2,1,0:T(8,128)S(1)} %copy-done.1, f32[1,32,64,255]{3,2,1,0:T(8,128)S(1)} %get-tuple-element.192, f32[1,32,64,255]{3,2,1,0:T(8,128)S(1)} %get-tuple-element.193, ...), kind=kOutput, calls=%fused_computation.24.clone.1 | convolution fusion | flops 411566080 | bytes 16992256 | tf_op jit(solution)/shard_map/while/body/eval_jaxpr/zrp,gzsp->grs/dot_general | solution.py:58
  201.7 0.8 fusion.56
  202.5 0.8 fusion.57
  203.7 0.4 copy-done
  204.1 0.6 copy-done.1
  204.7 0.6 copy-done.2
  205.4 3.3 %fusion.61 = f32[1,1,64,64]{2,3,1,0:T(8,128)S(1)} fusion(f32[32,64,256]{2,1,0:T(8,128)S(1)} %copy-done.2, f32[32,64,256]{2,1,0:T(8,128)S(1)} %copy-done, f32[32,64,256]{2,1,0:T(8,128)S(1)} %copy-done.1, f32[1,32,64,255]{3,2,1,0:T(8,128)S(1)} %get-tuple-element.192, f32[1,32,64,255]{3,2,1,0:T(8,128)S(1)} %get-tuple-element.193, ...), kind=kOutput, calls=%fused_computation.24.clone.1 | convolution fusion | flops 411566080 | bytes 16992256 | tf_op jit(solution)/shard_map/while/body/eval_jaxpr/zrp,gzsp->grs/dot_general | solution.py:58
  209.0 0.8 fusion.56
  209.8 0.8 fusion.57
  211.0 0.4 copy-done
  211.4 0.6 copy-done.1
  212.0 0.6 copy-done.2
  212.7 3.3 %fusion.61 = f32[1,1,64,64]{2,3,1,0:T(8,128)S(1)} fusion(f32[32,64,256]{2,1,0:T(8,128)S(1)} %copy-done.2, f32[32,64,256]{2,1,0:T(8,128)S(1)} %copy-done, f32[32,64,256]{2,1,0:T(8,128)S(1)} %copy-done.1, f32[1,32,64,255]{3,2,1,0:T(8,128)S(1)} %get-tuple-element.192, f32[1,32,64,255]{3,2,1,0:T(8,128)S(1)} %get-tuple-element.193, ...), kind=kOutput, calls=%fused_computation.24.clone.1 | convolution fusion | flops 411566080 | bytes 16992256 | tf_op jit(solution)/shard_map/while/body/eval_jaxpr/zrp,gzsp->grs/dot_general | solution.py:58
  216.3 0.8 fusion.56
  217.1 0.8 fusion.57
  218.3 0.4 copy-done
  218.7 0.6 copy-done.1
  219.3 0.6 copy-done.2
  220.0 3.3 %fusion.61 = f32[1,1,64,64]{2,3,1,0:T(8,128)S(1)} fusion(f32[32,64,256]{2,1,0:T(8,128)S(1)} %copy-done.2, f32[32,64,256]{2,1,0:T(8,128)S(1)} %copy-done, f32[32,64,256]{2,1,0:T(8,128)S(1)} %copy-done.1, f32[1,32,64,255]{3,2,1,0:T(8,128)S(1)} %get-tuple-element.192, f32[1,32,64,255]{3,2,1,0:T(8,128)S(1)} %get-tuple-element.193, ...), kind=kOutput, calls=%fused_computation.24.clone.1 | convolution fusion | flops 411566080 | bytes 16992256 | tf_op jit(solution)/shard_map/while/body/eval_jaxpr/zrp,gzsp->grs/dot_general | solution.py:58
  223.6 0.8 fusion.56
  224.4 0.8 fusion.57
  225.6 0.4 copy-done
  226.0 0.6 copy-done.1
  226.6 0.6 copy-done.2
  227.3 3.3 %fusion.61 = f32[1,1,64,64]{2,3,1,0:T(8,128)S(1)} fusion(f32[32,64,256]{2,1,0:T(8,128)S(1)} %copy-done.2, f32[32,64,256]{2,1,0:T(8,128)S(1)} %copy-done, f32[32,64,256]{2,1,0:T(8,128)S(1)} %copy-done.1, f32[1,32,64,255]{3,2,1,0:T(8,128)S(1)} %get-tuple-element.192, f32[1,32,64,255]{3,2,1,0:T(8,128)S(1)} %get-tuple-element.193, ...), kind=kOutput, calls=%fused_computation.24.clone.1 | convolution fusion | flops 411566080 | bytes 16992256 | tf_op jit(solution)/shard_map/while/body/eval_jaxpr/zrp,gzsp->grs/dot_general | solution.py:58
  230.9 0.8 fusion.56
  231.7 0.8 fusion.57
  232.9 0.4 copy-done
  233.3 0.6 copy-done.1
  233.9 0.6 copy-done.2
  234.6 3.3 %fusion.61 = f32[1,1,64,64]{2,3,1,0:T(8,128)S(1)} fusion(f32[32,64,256]{2,1,0:T(8,128)S(1)} %copy-done.2, f32[32,64,256]{2,1,0:T(8,128)S(1)} %copy-done, f32[32,64,256]{2,1,0:T(8,128)S(1)} %copy-done.1, f32[1,32,64,255]{3,2,1,0:T(8,128)S(1)} %get-tuple-element.192, f32[1,32,64,255]{3,2,1,0:T(8,128)S(1)} %get-tuple-element.193, ...), kind=kOutput, calls=%fused_computation.24.clone.1 | convolution fusion | flops 411566080 | bytes 16992256 | tf_op jit(solution)/shard_map/while/body/eval_jaxpr/zrp,gzsp->grs/dot_general | solution.py:58
  238.2 0.8 fusion.56
  239.0 0.8 fusion.57
  240.2 0.4 copy-done
  240.6 0.6 copy-done.1
  241.2 0.6 copy-done.2
  241.9 3.3 %fusion.61 = f32[1,1,64,64]{2,3,1,0:T(8,128)S(1)} fusion(f32[32,64,256]{2,1,0:T(8,128)S(1)} %copy-done.2, f32[32,64,256]{2,1,0:T(8,128)S(1)} %copy-done, f32[32,64,256]{2,1,0:T(8,128)S(1)} %copy-done.1, f32[1,32,64,255]{3,2,1,0:T(8,128)S(1)} %get-tuple-element.192, f32[1,32,64,255]{3,2,1,0:T(8,128)S(1)} %get-tuple-element.193, ...), kind=kOutput, calls=%fused_computation.24.clone.1 | convolution fusion | flops 411566080 | bytes 16992256 | tf_op jit(solution)/shard_map/while/body/eval_jaxpr/zrp,gzsp->grs/dot_general | solution.py:58
  245.3 0.8 reshape.125
  246.1 62.6 %reduce-scatter.2.cloned.1.call-done = f32[8,256]{1,0:T(8,128)} async-done(((f32[8,4096]{1,0:T(8,128)}), f32[8,256]{1,0:T(8,128)}) %reduce-scatter.2.cloned.1.call-update) | async-done | bytes 8208 | tf_op jit(solution)/shard_map/reduce_scatter | solution.py:73
  (118 shorter events, 4.5 us)
Async XLA Ops:
  6.5 94.8 %all-gather.3.cloned.1.call-start = ((), (), s32[]{:S(2)}) async-start(), calls=%async_computation.1 | async-start | bytes 2162688 | tf_op jit(solution)/shard_map/all_gather | solution.py:67
  7.3 179.7 %all-gather.5.cloned.1.call-start = ((), (), s32[]{:S(2)}) async-start(), calls=%async_computation.2 | async-start | bytes 2162688 | tf_op jit(solution)/shard_map/all_gather | solution.py:68
  8.0 95.0 %copy-start.6 = (f32[32,8,256]{2,1,0:T(8,128)S(1)}, f32[32,8,256]{2,1,0:T(8,128)}, u32[]{:S(2)}) copy-start(f32[32,8,256]{2,1,0:T(8,128)} %param.7) | copy-start | bytes 786436
  8.0 300.7 %reduce-scatter.2.cloned.1.call-start = ((), (), s32[]{:S(2)}) async-start(), calls=%async_computation.3 | async-start | bytes 139264 | tf_op jit(solution)/shard_map/reduce_scatter | solution.py:73
  103.1 1.4 copy-start.3
  104.5 4.4 %collective-permute-start.1 = (f32[1,72,256]{2,1,0:T(8,128)S(1)}, f32[1,72,256]{2,1,0:T(8,128)S(1)}, u32[]{:S(2)}, u32[]{:S(2)}) collective-permute-start(f32[1,72,256]{2,1,0:T(8,128)S(1)} %get-tuple-element.131), channel_id=1, source_target_pairs={{32,0},{64,32},{96,64},{128,96},{160,128},{192,160},{224,192},{256... | collective-permute-start | bytes 221192 | tf_op jit(solution)/shard_map/ppermute | solution.py:17
  105.8 3.9 %collective-permute-start = (f32[1,72,256]{2,1,0:T(8,128)S(1)}, f32[1,72,256]{2,1,0:T(8,128)S(1)}, u32[]{:S(2)}, u32[]{:S(2)}) collective-permute-start(f32[1,72,256]{2,1,0:T(8,128)S(1)} %get-tuple-element.130), channel_id=1, source_target_pairs={{0,32},{32,64},{64,96},{96,128},{128,160},{160,192},{192,224},{224... | collective-permute-start | bytes 221192 | tf_op jit(solution)/shard_map/ppermute | solution.py:14
  108.9 1.9 copy-start.4
  110.7 1.6 copy-start.5
  187.9 1.6 copy-start
  187.9 2.2 copy-start.1
  187.9 2.8 copy-start.2
  195.2 1.6 copy-start
  195.2 2.2 copy-start.1
  195.2 2.8 copy-start.2
  202.5 1.6 copy-start
  202.5 2.2 copy-start.1
  202.5 2.8 copy-start.2
  209.8 1.6 copy-start
  209.8 2.2 copy-start.1
  209.8 2.8 copy-start.2
  217.1 1.6 copy-start
  217.1 2.2 copy-start.1
  217.1 2.8 copy-start.2
  224.4 1.6 copy-start
  224.4 2.2 copy-start.1
  224.4 2.8 copy-start.2
  231.7 1.6 copy-start
  231.7 2.2 copy-start.1
  231.7 2.8 copy-start.2
  239.0 1.6 copy-start
  239.0 2.2 copy-start.1
  239.0 2.8 copy-start.2
Sparse Core Ops, SparseCore 0:
  10.5 90.7 all-gather.2
  104.5 82.4 all-gather.4
  246.2 62.4 reduce-scatter.1
where the time goes:
time: 315 us
  waiting for transfers between devices  230 us (73%)
  local copies, waits for them, and re-layouts  35.1 us (11%)
  matrix products  26.7 us (8%)
  between operations  13.2 us (4%)
  other arithmetic  4.6 us (1%)
  starting transfers between devices  4.4 us (1%)
    all_gather x1, waiting for transfers between devices, local(): lax.all_gather(right_modes, 'term', axis=0, tiled=True)  93.2 us
    all_gather x1, waiting for transfers between devices, local(): lax.all_gather(adjoint_modes, 'term', axis=0, tiled=True)  72.1 us
    reduce_scatter x1, waiting for transfers between devices, local(): lax.psum_scatter(partial_value, 'space', scatter_dimension=1, tiled=True)  62.6 us
    dot_general x8, matrix products, one_block(): jnp.einsum('zrp,gzsp->grs', adjoint, image, precision=lax.Precision.HIGHEST)  26.7 us
    slice x32, local copies, waits for them, and re-layouts, shifted_cells(): return jnp.concatenate([values[..., offset:], zeros], axis=-1)  14 us
    while x48, local copies, waits for them, and re-layouts  13.6 us
  transfers between devices with their start and end apart: 5, of which 4 were waited for; matrix products, arithmetic and copies ran while one was open for 2% of the time, Pallas kernels for 0%

commit v1 on v0

v1 whole, which is shorter than its diff:
```python
import jax
import jax.numpy as jnp
from jax import lax
from jax.experimental import pallas as pl
from jax.experimental.pallas import tpu as pltpu
from jax.sharding import PartitionSpec as P

MESH = pl.DeviceIdType.MESH
GY = 32
NX, NL, NC = 4, 2, 2
NZ, NH = 8, 4
VMEM = pl.BlockSpec(memory_space=pltpu.VMEM)


def remote(src, dst, send, recv, space, term):
    return pltpu.make_async_remote_copy(
        src_ref=src, dst_ref=dst, send_sem=send, recv_sem=recv,
        device_id=(space, term), device_id_type=MESH,
    )


def gather_kernel(right_ref, adjoint_ref, coeff_ref, field_ref, terms_ref, send_sem, recv_sem, term_send, term_recv):
    spaces, terms = NX * NL * NC, NZ * NH
    space, term = lax.axis_index("space"), lax.axis_index("term")
    z, h = lax.div(term, NH), lax.rem(term, NH)
    after = z * NH + lax.rem(h + 1, NH)
    before = z * NH + lax.rem(h + NH - 1, NH)
    up = (lax.rem(space + jnp.where(z == NZ - 1, 1, 0), spaces), lax.rem(term + NH, terms))
    down = (lax.rem(space + jnp.where(z == 0, spaces - 1, 0), spaces), lax.rem(term + terms - NH, terms))
    column = [lax.rem(z + step, NZ) for step in range(1, NZ)]

    barrier = pltpu.get_barrier_semaphore()
    partners = [(space, after), (space, before), up, down] + [(space, other * NH + h) for other in column]
    for partner in partners:
        pl.semaphore_signal(barrier, inc=1, device_id=partner, device_id_type=MESH)
    pl.semaphore_wait(barrier, len(partners))

    own = h + 1
    sources = (adjoint_ref.at[0], right_ref.at[0])

    def field(slot, kind, source, number, target):
        return remote(source, field_ref.at[slot, kind], send_sem.at[number], recv_sem.at[slot, kind], *target)

    def held(slot, kind, number, target):
        return field(slot, kind, field_ref.at[slot, kind], number, target)

    def arrival(slot, kind):
        pltpu.make_async_copy(field_ref.at[slot, kind], field_ref.at[slot, kind], recv_sem.at[slot, kind]).wait()

    first = []
    for kind in (0, 1):
        first.append(field(own, kind, sources[kind], kind, (space, after)))
        first.append(field(own, kind, sources[kind], 2 + kind, (space, before)))
    to_up = [field(0, kind, sources[kind], 4 + kind, up) for kind in (0, 1)]
    to_down = [field(NH + 1, kind, sources[kind], 4 + kind, down) for kind in (0, 1)]

    @pl.when(h == NH - 1)
    def _():
        for copy in to_up:
            copy.start()

    @pl.when(h == 0)
    def _():
        for copy in to_down:
            copy.start()

    for copy in first:
        copy.start()
    coeff = []
    for step, other in enumerate(column):
        coeff.append(remote(
            coeff_ref.at[pl.ds(other * NH, NH)], terms_ref.at[z], term_send.at[step], term_recv.at[step],
            space, other * NH + h,
        ))
        coeff[-1].start()
    for kind in (0, 1):
        field_ref[own, kind] = sources[kind][...]
    terms_ref[z] = coeff_ref[pl.ds(z * NH, NH)]

    side = ((0, NH - 1, 0, 2), (NH + 1, 0, 2, 0))
    slot_before, slot_after = lax.rem(h + NH - 1, NH) + 1, lax.rem(h + 1, NH) + 1
    opposite = lax.rem(h + 2, NH) + 1

    low = [held(0, kind, 8 + kind, (space, after)) for kind in (0, 1)]
    low += [held(0, kind, 10 + kind, (space, before)) for kind in (0, 1)]
    high = [held(NH + 1, kind, 8 + kind, (space, after)) for kind in (0, 1)]
    high += [held(NH + 1, kind, 10 + kind, (space, before)) for kind in (0, 1)]

    @pl.when(h == NH - 1)
    def _():
        for kind in (0, 1):
            arrival(0, kind)
        for copy in low:
            copy.start()

    @pl.when(h == 0)
    def _():
        for kind in (0, 1):
            arrival(NH + 1, kind)
        for copy in high:
            copy.start()

    arrival(slot_before, 0)
    on_after = held(slot_before, 0, 6, (space, after))
    on_after.start()
    arrival(slot_after, 1)
    on_before = held(slot_after, 1, 7, (space, before))
    on_before.start()

    last = {
        0: [held(0, 1, 12, (space, after))],
        1: [held(NH + 1, 0, 12, (space, after))],
        2: [held(0, 0, 12, (space, before))],
        3: [held(NH + 1, 1, 12, (space, before))],
    }
    entered = {0: NH + 1, 3: 0}
    for which in range(NH):
        @pl.when(h == which)
        def _(which=which):
            for copy in last[which]:
                slot, kind = {0: (0, 1), 1: (NH + 1, 0), 2: (0, 0), 3: (NH + 1, 1)}[which]
                arrival(slot, kind)
                copy.start()
            done = {{0: (0, 1), 1: (NH + 1, 0), 2: (0, 0), 3: (NH + 1, 1)}[which]}
            if which in entered:
                done |= {(entered[which], 0), (entered[which], 1)}
            for slot in (0, NH + 1):
                for kind in (0, 1):
                    if (slot, kind) not in done:
                        arrival(slot, kind)
            for copy in last[which]:
                copy.wait_send()

    arrival(slot_before, 1)
    arrival(slot_after, 0)
    for kind in (0, 1):
        arrival(opposite, kind)
    for copy in coeff:
        copy.wait()
    for copy in first + [on_after, on_before]:
        copy.wait_send()

    @pl.when(h == NH - 1)
    def _():
        for copy in to_up + low:
            copy.wait_send()

    @pl.when(h == 0)
    def _():
        for copy in to_down + high:
            copy.wait_send()


def moved(values, shift, keep):
    return jnp.where(keep, pltpu.roll(values, shift % values.shape[-1], values.ndim - 1), 0.0)


def multiply_kernel(field_ref, terms_ref, out_ref, diff, weights):
    space, term = lax.axis_index("space"), lax.axis_index("term")
    z = lax.div(term, NH)
    lowest = jnp.logical_and(space == 0, z == 0)
    highest = jnp.logical_and(space == NX * NL * NC - 1, z == NZ - 1)
    modes, plane = field_ref.shape[2:]
    cell = lax.broadcasted_iota(jnp.int32, (modes, plane), 1)
    column = lax.rem(cell, GY)
    keeps = ((GY, cell >= GY), (-GY, cell < plane - GY), (1, column != 0), (-1, column != GY - 1))
    for kind in (0, 1):
        for slot in range(NH + 1):
            below, above = field_ref[slot, kind], field_ref[slot + 1, kind]
            if slot == 0:
                below = jnp.where(lowest, 0.0, below)
            if slot == NH:
                above = jnp.where(highest, 0.0, above)
            diff[kind, slot] = above - below
        for slot in range(NH):
            own = field_ref[slot + 1, kind]
            for which, (shift, keep) in enumerate(keeps):
                diff[kind, NH + 1 + NH * which + slot] = own - moved(own, shift, keep)
    for slot in range(NH):
        value = 0.5 * terms_ref[:, slot].reshape(modes, plane)
        high = value.astype(jnp.bfloat16)
        rest = (value - high.astype(jnp.float32)).astype(jnp.bfloat16)
        weights[:, slot * plane:(slot + 1) * plane] = jnp.concatenate([high, rest], axis=0)

    lanes = lax.broadcasted_iota(jnp.int32, (modes, 2 * modes), 1)

    def product(row, index):
        return diff[0, index, pl.ds(row, 1), :] * diff[1, index]

    def step(turn, carry):
        d, j0 = lax.div(turn, 2), lax.rem(turn, 2)
        folded = []
        for j1 in (0, 1):
            row = 4 * d + 2 * j1 + j0
            total = None
            edge = product(row, 0)
            for slot in range(NH):
                upper = product(row, slot + 1)
                value = edge + upper
                edge = upper
                for which in range(4):
                    value = value + product(row, NH + 1 + NH * which + slot)
                high = value.astype(jnp.bfloat16)
                rest = (value - high.astype(jnp.float32)).astype(jnp.bfloat16)
                part = lax.dot_general(
                    jnp.concatenate([high, rest], axis=0), weights[:, slot * plane:(slot + 1) * plane],
                    (((1,), (1,)), ((), ())), preferred_element_type=jnp.float32,
                )
                total = part if total is None else total + part
            total = total[:modes] + total[modes:]
            folded.append(total + pltpu.roll(total, modes, 1))
        out_ref[d, pl.ds(pl.multiple_of(j0 * modes, modes), modes), :] = jnp.where(lanes < modes, folded[0], folded[1])
        return carry

    lax.fori_loop(0, out_ref.shape[0] * 2, step, 0)


def reduce_kernel(part_ref, out_ref, pair_in, mine, slab_in, turned, column_in, pair_sem, slab_sem, column_sem):
    space, term = lax.axis_index("space"), lax.axis_index("term")
    c = lax.rem(space, NC)
    x, l = lax.div(space, NL * NC), lax.rem(lax.div(space, NC), NL)
    z, h = lax.div(term, NH), lax.rem(term, NH)
    places = []
    for dx, dl in ((2, 1), (1, 1), (3, 1), (2, 0), (1, 0), (3, 0), (0, 1), (0, 0)):
        places.append(lax.rem(x + dx, NX) * NL + lax.rem(l + dl, NL))
    column = [lax.rem(z + step, NZ) for step in range(1, NZ)]
    other_core = places[-1] * NC + 1 - c

    barrier = pltpu.get_barrier_semaphore()
    partners = [(other_core, term)] + [(place * NC + c, term) for place in places[:-1]]
    partners += [(space, other * NH + h) for other in column]
    for partner in partners:
        pl.semaphore_signal(barrier, inc=1, device_id=partner, device_id_type=MESH)
    pl.semaphore_wait(barrier, len(partners))

    pair = []
    for number, place in enumerate(places):
        pair.append(remote(
            part_ref.at[place * NC + 1 - c], pair_in.at[number], pair_sem.at[0, number], pair_sem.at[1, number],
            other_core, term,
        ))
        pair[-1].start()
    slab = []
    for number, place in enumerate(places):
        pair[number].wait_recv()
        mine[number] = part_ref[place * NC + c] + pair_in[number]
        if number < len(places) - 1:
            slab.append(remote(
                mine.at[number], slab_in.at[number], slab_sem.at[0, number], slab_sem.at[1, number],
                place * NC + c, term,
            ))
            slab[-1].start()
    total = mine[len(places) - 1]
    for number, copy in enumerate(slab):
        copy.wait_recv()
        total = total + slab_in[number]
    total = total.T
    turned[...] = total.reshape(turned.shape)
    sent = []
    for step, other in enumerate(column):
        sent.append(remote(
            turned.at[:, other], column_in.at[step], column_sem.at[0, step], column_sem.at[1, step],
            space, other * NH + h,
        ))
        sent[-1].start()
    result = turned[:, z]
    for step, copy in enumerate(sent):
        copy.wait_recv()
        result = result + column_in[step]
    width = result.shape[-1]
    out_ref[:, :width] = result[0]
    out_ref[:, width:] = result[1]
    for copy in pair + slab + sent:
        copy.wait_send()


def local(right_modes, adjoint_modes, conductivity_terms):
    modes, plane = right_modes.shape[1:]
    per = conductivity_terms.shape[1]
    spaces = NX * NL * NC
    field, terms = pl.pallas_call(
        gather_kernel,
        out_shape=(
            jax.ShapeDtypeStruct((NH + 2, 2, modes, plane), jnp.float32),
            jax.ShapeDtypeStruct((NZ, NH, per, plane), jnp.float32),
        ),
        in_specs=[VMEM] * 3,
        out_specs=(VMEM, VMEM),
        scratch_shapes=[
            pltpu.SemaphoreType.DMA((13,)),
            pltpu.SemaphoreType.DMA((NH + 2, 2)),
            pltpu.SemaphoreType.DMA((NZ - 1,)),
            pltpu.SemaphoreType.DMA((NZ - 1,)),
        ],
        compiler_params=pltpu.CompilerParams(collective_id=0, has_side_effects=True),
        name="gather_planes",
    )(right_modes, adjoint_modes, conductivity_terms)
    part = pl.pallas_call(
        multiply_kernel,
        out_shape=jax.ShapeDtypeStruct((spaces, 2 * modes, 2 * modes), jnp.float32),
        in_specs=[VMEM] * 2,
        out_specs=VMEM,
        scratch_shapes=[
            pltpu.VMEM((2, 5 * NH + 1, modes, plane), jnp.float32),
            pltpu.VMEM((2 * modes, NH * plane), jnp.bfloat16),
        ],
        name="multiply_planes",
    )(field, terms)
    return pl.pallas_call(
        reduce_kernel,
        out_shape=jax.ShapeDtypeStruct((per, 4 * modes), jnp.float32),
        in_specs=[VMEM],
        out_specs=VMEM,
        scratch_shapes=[
            pltpu.VMEM((NX * NL, 2 * modes, 2 * modes), jnp.float32),
            pltpu.VMEM((NX * NL, 2 * modes, 2 * modes), jnp.float32),
            pltpu.VMEM((NX * NL - 1, 2 * modes, 2 * modes), jnp.float32),
            pltpu.VMEM((2, NZ, per, 2 * modes), jnp.float32),
            pltpu.VMEM((NZ - 1, 2, per, 2 * modes), jnp.float32),
            pltpu.SemaphoreType.DMA((2, NX * NL)),
            pltpu.SemaphoreType.DMA((2, NX * NL - 1)),
            pltpu.SemaphoreType.DMA((2, NZ - 1)),
        ],
        compiler_params=pltpu.CompilerParams(collective_id=1, has_side_effects=True),
        name="reduce_parts",
    )(part)


def solution(mesh):
    placed = (
        P(("space", "term"), None, None),
        P(("space", "term"), None, None),
        P("space", "term", None),
    )
    return jax.shard_map(
        local, mesh=mesh, in_specs=placed, out_specs=P("term", "space"), check_vma=False
    )
```

time: 315 us -> 73.6 us (0.23)
  the two profiles are of different devices: /device:TPU:16 before, /device:TPU:20 now
where the time goes in v1:
time: 73.6 us; the launch traced here: 73.3 us
  Pallas kernels  72 us (98%)
  local copies, waits for them, and re-layouts  1.3 us (2%)
    pallas_call x1, Pallas kernels, local(): pl.pallas_call(gather_kernel, out_shape=(jax.ShapeDtypeStruct((NH + 2, 2,...  31.8 us
    pallas_call x1, Pallas kernels, local(): pl.pallas_call(reduce_kernel, out_shape=jax.ShapeDtypeStruct((per, 4 * mo...  22 us
    pallas_call x1, Pallas kernels, local(): pl.pallas_call(multiply_kernel, out_shape=jax.ShapeDtypeStruct((spaces, 2...  18.2 us

profile of v1, /device:TPU:20, one launch (start us, length us, event | category | flops | bytes accessed | tf_op | source)
XLA Modules:
  0.0 73.3 jit_solution(2930423894801012879)
XLA Ops:
  0.0 31.8 %gather_planes.1 = (f32[6,2,64,256]{3,2,1,0:T(8,128)}, f32[8,4,8,256]{3,2,1,0:T(8,128)}) custom-call(f32[1,64,256]{2,1,0:T(8,128)} %right_ref.1, f32[1,64,256]{2,1,0:T(8,128)} %adjoint_ref.1, f32[32,8,256]{2,1,0:T(8,128)} %coeff_ref.1), custom_call_target="tpu_custom_call" | custom-call | tf_op jit(solution)/shard_map/gather_planes/pallas_call | solution.py:281
  31.8 18.2 %multiply_planes.1.part_ref = f32[16,128,128]{2,1,0:T(8,128)} custom-call(f32[6,2,64,256]{3,2,1,0:T(8,128)} %get-tuple-element.7.field_ref, f32[8,4,8,256]{3,2,1,0:T(8,128)} %get-tuple-element.8.terms_ref), custom_call_target="tpu_custom_call" | custom-call | tf_op jit(solution)/shard_map/multiply_planes/pallas_call | solution.py:298
  50.0 22.0 %reduce_parts.1 = f32[8,256]{1,0:T(8,128)} custom-call(f32[16,128,128]{2,1,0:T(8,128)} %multiply_planes.1.part_ref), custom_call_target="tpu_custom_call" | custom-call | tf_op jit(solution)/shard_map/reduce_parts/pallas_call | solution.py:309
  72.0 1.3 %copy.5 = f32[8,256]{1,0:T(8,128)} copy(f32[8,256]{1,0:T(8,128)} %reduce_parts.1) | data formatting | bytes 16384

commit v2 on v0

v2 whole, which is shorter than its diff:
```python
import jax
import jax.numpy as jnp
from jax import lax
from jax.experimental import pallas as pl
from jax.experimental.pallas import tpu as pltpu
from jax.sharding import PartitionSpec as P

MESH = pl.DeviceIdType.MESH
GY = 32
NX, NL, NC = 4, 2, 2
NZ, NH = 8, 4
VMEM = pl.BlockSpec(memory_space=pltpu.VMEM)


def moved(values, shift, keep):
    return jnp.where(keep, pltpu.roll(values, shift % values.shape[-1], values.ndim - 1), 0.0)


def assemble_kernel(
    right_ref, adjoint_ref, coeff_ref, out_ref,
    field, terms, flat, edges, weights, part, pair_in, mine, slab_in, turned, column_in,
    send_sem, recv_sem, term_sem, pair_sem, slab_sem, column_sem,
):
    spaces, total_terms, places = NX * NL * NC, NZ * NH, NX * NL
    modes, plane = right_ref.shape[1:]
    space, term = lax.axis_index("space"), lax.axis_index("term")
    c = lax.rem(space, NC)
    x, l = lax.div(space, NL * NC), lax.rem(lax.div(space, NC), NL)
    z, h = lax.div(term, NH), lax.rem(term, NH)
    after = (space, z * NH + lax.rem(h + 1, NH))
    before = (space, z * NH + lax.rem(h + NH - 1, NH))
    up = (lax.rem(space + jnp.where(z == NZ - 1, 1, 0), spaces), lax.rem(term + NH, total_terms))
    down = (lax.rem(space + jnp.where(z == 0, spaces - 1, 0), spaces), lax.rem(term + total_terms - NH, total_terms))
    column = [lax.rem(z + step, NZ) for step in range(1, NZ)]

    def place(n):
        return lax.rem(x + lax.rem(n + 1, NX), NX) * NL + lax.rem(l + NL - 1 - lax.div(n, NX), NL)

    def remote(src, dst, send, recv, target):
        return pltpu.make_async_remote_copy(
            src_ref=src, dst_ref=dst, send_sem=send, recv_sem=recv, device_id=target, device_id_type=MESH,
        )

    barrier = pltpu.get_barrier_semaphore()
    partners = [after, before, up, down] + [(space, other * NH + h) for other in column]
    partners += [(place(n) * NC + c, term) for n in range(places - 1)]
    partners += [(place(places - 1) * NC + 1 - c, term)]
    for partner in partners:
        pl.semaphore_signal(barrier, inc=1, device_id=partner, device_id_type=MESH)
    pl.semaphore_wait(barrier, len(partners))

    own, top = h + 1, NH + 1
    slot_before, slot_after = lax.rem(h + NH - 1, NH) + 1, lax.rem(h + 1, NH) + 1
    opposite = lax.rem(h + 2, NH) + 1
    sources = (adjoint_ref.at[0], right_ref.at[0])

    def fresh(slot, kind, number, target):
        return remote(sources[kind], field.at[slot, kind], send_sem.at[number], recv_sem.at[slot, kind], target)

    def held(slot, kind, number, target):
        return remote(
            field.at[slot, kind], field.at[slot, kind], send_sem.at[number], recv_sem.at[slot, kind], target
        )

    def arrival(slot, kind):
        pltpu.make_async_copy(field.at[slot, kind], field.at[slot, kind], recv_sem.at[slot, kind]).wait()

    coeff = []
    for step, other in enumerate(column):
        coeff.append(remote(
            coeff_ref.at[pl.ds(other * NH, NH)], terms.at[z], term_sem.at[0, step], term_sem.at[1, step],
            (space, other * NH + h),
        ))
    first = [fresh(own, 0, 0, after), fresh(own, 1, 1, before), fresh(own, 1, 2, after), fresh(own, 0, 3, before)]
    to_up = [fresh(0, kind, 4 + kind, up) for kind in (0, 1)]
    to_down = [fresh(top, kind, 4 + kind, down) for kind in (0, 1)]
    low = [held(0, 0, 8, after), held(0, 1, 9, before), held(0, 1, 10, after), held(0, 0, 11, before)]
    high = [held(top, 0, 8, after), held(top, 1, 9, before), held(top, 1, 10, after), held(top, 0, 11, before)]
    low_on = [held(0, kind, 8 + kind, before) for kind in (0, 1)]
    high_on = [held(top, kind, 8 + kind, after) for kind in (0, 1)]
    on_after, on_before = held(slot_before, 0, 6, after), held(slot_after, 1, 7, before)

    for copy in first[:2]:
        copy.start()

    @pl.when(h == NH - 1)
    def _():
        for copy in to_up:
            copy.start()

    @pl.when(h == 0)
    def _():
        for copy in to_down:
            copy.start()

    for copy in first[2:] + coeff:
        copy.start()
    terms[z] = coeff_ref[pl.ds(z * NH, NH)]

    cell = lax.broadcasted_iota(jnp.int32, (modes, plane), 1)
    in_row = lax.rem(cell, GY)
    keeps = ((GY, cell >= GY), (-GY, cell < plane - GY), (1, in_row != 0), (-1, in_row != GY - 1))

    def flatten(which, kind, values):
        for number, (shift, keep) in enumerate(keeps):
            flat[kind, 4 * which + number] = values - moved(values, shift, keep)

    for kind in (0, 1):
        values = sources[kind][...]
        field[own, kind] = values
        flatten(0, kind, values)

    @pl.when(h == NH - 1)
    def _():
        for kind in (0, 1):
            arrival(0, kind)
        for copy in low:
            copy.start()

    @pl.when(h == 0)
    def _():
        for kind in (0, 1):
            arrival(top, kind)
        for copy in high:
            copy.start()

    for copy in coeff:
        copy.wait_recv()
    for slot in range(NH):
        value = 0.5 * terms[:, slot].reshape(-1, plane)
        upper = value.astype(jnp.bfloat16)
        lower = (value - upper.astype(jnp.float32)).astype(jnp.bfloat16)
        weights[slot] = jnp.concatenate([upper, lower], axis=0)

    arrival(slot_before, 0)
    on_after.start()
    arrival(slot_after, 1)
    on_before.start()
    arrival(slot_before, 1)
    arrival(slot_after, 0)
    for which, slot in ((1, slot_after), (2, slot_before)):
        for kind in (0, 1):
            flatten(which, kind, field[slot, kind])

    @pl.when(h == 1)
    def _():
        for kind in (0, 1):
            arrival(top, kind)
        for copy in high_on:
            copy.start()

    @pl.when(h == 2)
    def _():
        for kind in (0, 1):
            arrival(0, kind)
        for copy in low_on:
            copy.start()

    lanes = lax.broadcasted_iota(jnp.int32, (modes, 2 * modes), 1)

    def times(value, weight):
        upper = value.astype(jnp.bfloat16)
        lower = (value - upper.astype(jnp.float32)).astype(jnp.bfloat16)
        return lax.dot_general(
            jnp.concatenate([upper, lower], axis=0), weight, (((1,), (1,)), ((), ())),
            preferred_element_type=jnp.float32,
        )

    def level(row, which):
        value = None
        for number in range(4 * which, 4 * which + 4):
            product = flat[0, number, pl.ds(row, 1), :] * flat[1, number]
            value = product if value is None else value + product
        return value

    def folded(totals):
        halves = []
        for total in totals:
            total = total[:modes] + total[modes:]
            halves.append(total + pltpu.roll(total, modes, 1))
        return jnp.where(lanes < modes, *halves)

    def near(turn, carry):
        d, j0 = lax.div(turn, 2), lax.rem(turn, 2)
        totals = []
        for j1 in (0, 1):
            row = 4 * d + 2 * j1 + j0
            total = times(level(row, 0), weights[own - 1])
            total += times(level(row, 1), weights[slot_after - 1])
            total += times(level(row, 2), weights[slot_before - 1])
            totals.append(total)
        part[d, pl.ds(pl.multiple_of(j0 * modes, modes), modes), :] = folded(totals)
        return carry

    lax.fori_loop(0, 2 * spaces, near, 0)

    @pl.when(jnp.logical_or(h == 0, h == NH - 1))
    def _():
        slot = jnp.where(h == 0, 0, top)
        for kind in (0, 1):
            arrival(slot, kind)

    @pl.when(h == 1)
    def _():
        for kind in (0, 1):
            arrival(0, kind)

    @pl.when(h == 2)
    def _():
        for kind in (0, 1):
            arrival(top, kind)

    for kind in (0, 1):
        arrival(opposite, kind)
        flatten(3, kind, field[opposite, kind])

    lowest = jnp.logical_and(space == 0, z == 0)
    highest = jnp.logical_and(space == spaces - 1, z == NZ - 1)
    for kind in (0, 1):
        for slot in range(NH + 1):
            lower, upper = field[slot, kind], field[slot + 1, kind]
            if slot == 0:
                lower = jnp.where(lowest, 0.0, lower)
            if slot == NH:
                upper = jnp.where(highest, 0.0, upper)
            edges[kind, slot] = upper - lower

    def far(d, j0):
        totals = []
        for j1 in (0, 1):
            row = 4 * d + 2 * j1 + j0
            total = times(level(row, 3), weights[opposite - 1])
            lower = edges[0, 0, pl.ds(row, 1), :] * edges[1, 0]
            for slot in range(NH):
                upper = edges[0, slot + 1, pl.ds(row, 1), :] * edges[1, slot + 1]
                total += times(lower + upper, weights[slot])
                lower = upper
            totals.append(total)
        rows = pl.ds(pl.multiple_of(j0 * modes, modes), modes)
        part[d, rows, :] = part[d, rows, :] + folded(totals)

    def pair(n):
        return remote(
            part.at[place(n) * NC + 1 - c], pair_in.at[n], pair_sem.at[0, n], pair_sem.at[1, n],
            (place(places - 1) * NC + 1 - c, term),
        )

    def slab(n):
        return remote(
            mine.at[n], slab_in.at[n], slab_sem.at[0, n], slab_sem.at[1, n], (place(n) * NC + c, term)
        )

    def join(n):
        pair(n).wait_recv()
        mine[n] = part[place(n) * NC + c] + pair_in[n]

    def turn(n, carry):
        def inner(k, carry):
            far(place(n) * NC + lax.rem(c + 1 + lax.div(k, 2), 2), lax.rem(k, 2))
            return carry

        lax.fori_loop(0, 4, inner, 0)
        pair(n).start()

        @pl.when(n > 0)
        def _():
            join(n - 1)
            slab(n - 1).start()

        return carry

    lax.fori_loop(0, places, turn, 0)
    join(places - 1)
    total = mine[places - 1]
    for n in range(places - 1):
        slab(n).wait_recv()
        total = total + slab_in[n]
    total = total.T
    turned[...] = total.reshape(turned.shape)
    sent = []
    for step, other in enumerate(column):
        sent.append(remote(
            turned.at[:, other], column_in.at[step], column_sem.at[0, step], column_sem.at[1, step],
            (space, other * NH + h),
        ))
        sent[-1].start()
    result = turned[:, z]
    for step, copy in enumerate(sent):
        copy.wait_recv()
        result = result + column_in[step]
    width = result.shape[-1]
    out_ref[:, :width] = result[0]
    out_ref[:, width:] = result[1]

    for copy in first + coeff + [on_after, on_before] + sent:
        copy.wait_send()
    for n in range(places):
        pair(n).wait_send()
    for n in range(places - 1):
        slab(n).wait_send()
    for which, copies in enumerate((to_down + high, high_on, low_on, to_up + low)):
        @pl.when(h == which)
        def _(copies=copies):
            for copy in copies:
                copy.wait_send()


def local(right_modes, adjoint_modes, conductivity_terms):
    modes, plane = right_modes.shape[1:]
    per = conductivity_terms.shape[1]
    spaces, places = NX * NL * NC, NX * NL
    block = (2 * modes, 2 * modes)
    return pl.pallas_call(
        assemble_kernel,
        out_shape=jax.ShapeDtypeStruct((per, 4 * modes), jnp.float32),
        in_specs=[VMEM] * 3,
        out_specs=VMEM,
        scratch_shapes=[
            pltpu.VMEM((NH + 2, 2, modes, plane), jnp.float32),
            pltpu.VMEM((NZ, NH, per, plane), jnp.float32),
            pltpu.VMEM((2, 4 * NH, modes, plane), jnp.float32),
            pltpu.VMEM((2, NH + 1, modes, plane), jnp.float32),
            pltpu.VMEM((NH, 2 * NZ * per, plane), jnp.bfloat16),
            pltpu.VMEM((spaces,) + block, jnp.float32),
            pltpu.VMEM((places,) + block, jnp.float32),
            pltpu.VMEM((places,) + block, jnp.float32),
            pltpu.VMEM((max(places - 1, 1),) + block, jnp.float32),
            pltpu.VMEM((2, NZ, per, 2 * modes), jnp.float32),
            pltpu.VMEM((max(NZ - 1, 1), 2, per, 2 * modes), jnp.float32),
            pltpu.SemaphoreType.DMA((12,)),
            pltpu.SemaphoreType.DMA((NH + 2, 2)),
            pltpu.SemaphoreType.DMA((2, max(NZ - 1, 1))),
            pltpu.SemaphoreType.DMA((2, places)),
            pltpu.SemaphoreType.DMA((2, max(places - 1, 1))),
            pltpu.SemaphoreType.DMA((2, max(NZ - 1, 1))),
        ],
        compiler_params=pltpu.CompilerParams(collective_id=0, has_side_effects=True),
        name="assemble_blocks",
    )(right_modes, adjoint_modes, conductivity_terms)


def solution(mesh):
    placed = (
        P(("space", "term"), None, None),
        P(("space", "term"), None, None),
        P("space", "term", None),
    )
    return jax.shard_map(
        local, mesh=mesh, in_specs=placed, out_specs=P("term", "space"), check_vma=False
    )
```

time: 315 us -> 65.3 us (0.21)
  waiting for transfers between devices: 230 us -> 0 us
  Pallas kernels: 0 us -> 63.8 us
  local copies, waits for them, and re-layouts: 35.1 us -> 1.3 us
  matrix products: 26.7 us -> 0 us
  between operations: 13.2 us -> 0.01 us
  other arithmetic: 4.6 us -> 0 us
  starting transfers between devices: 4.4 us -> 0 us
    all_gather x2 -> x0, waiting for transfers between devices: 165 us -> none  [the longest x1 93.2 us: local(): lax.all_gather(right_modes, 'term', axis=0, tiled=True)]
    pallas_call x0 -> x1, Pallas kernels: none -> 63.8 us  [local(): pl.pallas_call(assemble_kernel, out_shape=jax.ShapeDtypeStruct((per, 4 *...]
    reduce_scatter x1 -> x0, waiting for transfers between devices: 62.6 us -> none  [local(): lax.psum_scatter(partial_value, 'space', scatter_dimension=1, tiled=True)]
    dot_general x8 -> x0, matrix products: 26.7 us -> none  [one_block(): jnp.einsum('zrp,gzsp->grs', adjoint, image, precision=lax.Precision.HIGHEST)]
    slice x33 -> x0, local copies, waits for them, and re-layouts: 14 us -> none  [the longest x32 14 us: shifted_cells(): return jnp.concatenate([values[..., offset:], zeros], axis=-1)]
    while x48 -> x0, local copies, waits for them, and re-layouts: 13.6 us -> none
    ppermute x2 -> x0, starting transfers between devices: 4.33 us -> none  [the longest x1 3.03 us: extended(): lax.ppermute(lax.slice_in_dim(block, block.shape[dim] - width, None, axis...]
    unnamed x9 -> x1, local copies, waits for them, and re-layouts: 4.49 us -> 1.3 us
  transfers between devices with their start and end apart: 5 -> 0, of which waited for: 4 -> 0; matrix products, arithmetic and copies ran while one was open for 2% -> 0% of each run, Pallas kernels for 0% -> 0%
where the time goes in v2:
time: 65.3 us; the launch traced here: 65.1 us
  Pallas kernels  63.8 us (98%)
  local copies, waits for them, and re-layouts  1.3 us (2%)
    pallas_call x1, Pallas kernels, local(): pl.pallas_call(assemble_kernel, out_shape=jax.ShapeDtypeStruct((per, 4 *...  63.8 us

profile of v2, /device:TPU:16, one launch (start us, length us, event | category | flops | bytes accessed | tf_op | source)
XLA Modules:
  0.0 65.1 jit_solution(9122741774916919462)
XLA Ops:
  0.0 63.8 %assemble_blocks.1 = f32[8,256]{1,0:T(8,128)} custom-call(f32[1,64,256]{2,1,0:T(8,128)} %right_ref.1, f32[1,64,256]{2,1,0:T(8,128)} %adjoint_ref.1, f32[32,8,256]{2,1,0:T(8,128)} %coeff_ref.1), custom_call_target="tpu_custom_call" | custom-call | tf_op jit(solution)/shard_map/assemble_blocks/pallas_call | solution.py:313
  63.8 1.3 %copy.5 = f32[8,256]{1,0:T(8,128)} copy(f32[8,256]{1,0:T(8,128)} %assemble_blocks.1) | data formatting | bytes 16384

commit v3 on v0

v3 whole, which is shorter than its diff:
```python
import jax
import jax.numpy as jnp
from jax import lax
from jax.experimental import pallas as pl
from jax.experimental.pallas import tpu as pltpu
from jax.sharding import PartitionSpec as P

MESH = pl.DeviceIdType.MESH
GY = 32
NX, NL, NC = 4, 2, 2
NZ, NH = 8, 4
VMEM = pl.BlockSpec(memory_space=pltpu.VMEM)


def moved(values, shift, keep):
    return jnp.where(keep, pltpu.roll(values, shift % values.shape[-1], values.ndim - 1), 0.0)


def assemble_kernel(
    right_ref, adjoint_ref, coeff_ref, out_ref,
    field, terms, flat, edges, weights, part, pair_in, mine, slab_in, turned, column_in,
    send_sem, recv_sem, term_sem, pair_sem, slab_sem, column_sem,
):
    spaces, total_terms, places = NX * NL * NC, NZ * NH, NX * NL
    modes, plane = right_ref.shape[1:]
    space, term = lax.axis_index("space"), lax.axis_index("term")
    c = lax.rem(space, NC)
    x, l = lax.div(space, NL * NC), lax.rem(lax.div(space, NC), NL)
    z, h = lax.div(term, NH), lax.rem(term, NH)
    odd, mate = lax.rem(h, 2), NH - 1 - h
    index, planes = space * total_terms + term, spaces * total_terms

    def owner(number):
        return lax.div(number, total_terms), lax.rem(number, total_terms)

    above, below = owner(lax.rem(index + 1, planes)), owner(lax.rem(index + planes - 1, planes))
    partner_of_pair = owner(index + 1 - 2 * odd)
    owners = [(step, other) for step in range(NZ) for other in (0, 1)][1:]

    def holder(step, other):
        return lax.rem(z + step, NZ), (mate if other else h)

    def place(n):
        return lax.rem(x + lax.rem(n + 1, NX), NX) * NL + lax.rem(l + NL - 1 - lax.div(n, NX), NL)

    def remote(src, dst, send, recv, target):
        return pltpu.make_async_remote_copy(
            src_ref=src, dst_ref=dst, send_sem=send, recv_sem=recv, device_id=target, device_id_type=MESH,
        )

    barrier = pltpu.get_barrier_semaphore()
    partners = [above, below]
    for step, other in owners:
        far_z, far_h = holder(step, other)
        partners.append((space, far_z * NH + far_h))
    partners += [(place(n) * NC + c, term) for n in range(places - 1)]
    partners += [(place(places - 1) * NC + 1 - c, term)]
    for partner in partners:
        pl.semaphore_signal(barrier, inc=1, device_id=partner, device_id_type=MESH)
    pl.semaphore_wait(barrier, len(partners))

    own = 1 + odd
    sources = (adjoint_ref.at[0], right_ref.at[0])

    def fresh(slot, kind, number, target):
        return remote(sources[kind], field.at[slot, kind], send_sem.at[number], recv_sem.at[slot, kind], target)

    def arrival(slot, kind):
        pltpu.make_async_copy(field.at[slot, kind], field.at[slot, kind], recv_sem.at[slot, kind]).wait()

    first = [fresh(1 - odd, kind, kind, above) for kind in (0, 1)]
    first += [fresh(3 - odd, kind, 2 + kind, below) for kind in (0, 1)]
    relay = [
        remote(
            field.at[3 * odd, kind], field.at[3 * odd, kind], send_sem.at[4 + kind], recv_sem.at[3 * odd, kind],
            partner_of_pair,
        )
        for kind in (0, 1)
    ]
    coeff = []
    for number, (step, other) in enumerate(owners):
        far_z, far_h = holder(step, other)
        coeff.append(remote(
            coeff_ref.at[pl.ds(far_z * NH + 2 * lax.div(far_h, 2), 2)], terms.at[lax.div(h, 2), z],
            term_sem.at[0, number], term_sem.at[1, number], (space, far_z * NH + far_h),
        ))
    @pl.when(odd == 0)
    def _():
        for copy in (first[2], first[3], first[0], first[1]):
            copy.start()

    @pl.when(odd == 1)
    def _():
        for copy in first:
            copy.start()

    for copy in coeff:
        copy.start()
    terms[lax.div(h, 2), z] = coeff_ref[pl.ds(z * NH + 2 * lax.div(h, 2), 2)]

    cell = lax.broadcasted_iota(jnp.int32, (modes, plane), 1)
    in_row = lax.rem(cell, GY)
    keeps = ((GY, cell >= GY), (-GY, cell < plane - GY), (1, in_row != 0), (-1, in_row != GY - 1))

    def flatten(which, kind, values):
        for number, (shift, keep) in enumerate(keeps):
            flat[kind, 4 * which + number] = values - moved(values, shift, keep)

    for kind in (0, 1):
        values = sources[kind][...]
        field[own, kind] = values
        flatten(odd, kind, values)

    outer, inner, last = 3 * odd, 2 - odd, 3 - 3 * odd
    for kind in (0, 1):
        arrival(outer, kind)
        relay[kind].start()
    for copy in coeff:
        copy.wait_recv()
    for slot in (0, 1):
        value = 0.5 * terms[:, :, slot].reshape(-1, plane)
        upper = value.astype(jnp.bfloat16)
        lower = (value - upper.astype(jnp.float32)).astype(jnp.bfloat16)
        weights[:, slot * plane:(slot + 1) * plane] = jnp.concatenate([upper, lower], axis=0)
    for kind in (0, 1):
        arrival(inner, kind)
        flatten(1 - odd, kind, field[inner, kind])
    for kind in (0, 1):
        arrival(last, kind)

    lowest = jnp.logical_and(space == 0, term < 2)
    highest = jnp.logical_and(space == spaces - 1, term >= total_terms - 2)
    for kind in (0, 1):
        values = [field[slot, kind] for slot in range(4)]
        values[0] = jnp.where(lowest, 0.0, values[0])
        values[3] = jnp.where(highest, 0.0, values[3])
        for slot in range(3):
            edges[kind, slot] = values[slot + 1] - values[slot]

    count = weights.shape[0] // 2

    def assemble(d):
        left = []
        for row in range(4):
            row = 4 * d + row
            borders = [edges[0, slot, pl.ds(row, 1), :] * edges[1, slot] for slot in range(3)]
            values = []
            for slot in (0, 1):
                value = borders[slot] + borders[slot + 1]
                for number in range(4 * slot, 4 * slot + 4):
                    value = value + flat[0, number, pl.ds(row, 1), :] * flat[1, number]
                values.append(value)
            value = jnp.concatenate(values, axis=1)
            upper = value.astype(jnp.bfloat16)
            left += [upper, (value - upper.astype(jnp.float32)).astype(jnp.bfloat16)]
        total = lax.dot_general(
            jnp.concatenate(left, axis=0), weights[...], (((1,), (1,)), ((), ())), preferred_element_type=jnp.float32,
        )
        total = total[:, :count] + total[:, count:]
        for row in range(4):
            at = 2 * row * modes
            part[d, row * modes:(row + 1) * modes, :] = total[at:at + modes] + total[at + modes:at + 2 * modes]

    def pair(n):
        return remote(
            part.at[place(n) * NC + 1 - c], pair_in.at[n], pair_sem.at[0, n], pair_sem.at[1, n],
            (place(places - 1) * NC + 1 - c, term),
        )

    def slab(n):
        return remote(
            mine.at[n], slab_in.at[n], slab_sem.at[0, n], slab_sem.at[1, n], (place(n) * NC + c, term)
        )

    def join(n):
        pair(n).wait_recv()
        mine[n] = part[place(n) * NC + c] + pair_in[n]

    def turn(n, carry):
        def step(k, carry):
            assemble(place(n) * NC + lax.rem(c + 1 + k, 2))
            return carry

        lax.fori_loop(0, 2, step, 0)
        pair(n).start()

        @pl.when(n > 0)
        def _():
            join(n - 1)
            slab(n - 1).start()

        return carry

    lax.fori_loop(0, places, turn, 0)
    join(places - 1)
    total = mine[places - 1]
    for n in range(places - 1):
        slab(n).wait_recv()
        total = total + slab_in[n]
    total = total.T
    turned[...] = total.reshape(turned.shape)
    sent = []
    for number, (step, other) in enumerate(owners):
        far_z, far_h = holder(step, other)
        sent.append(remote(
            turned.at[lax.div(far_h, 2), far_z], column_in.at[number], column_sem.at[0, number],
            column_sem.at[1, number], (space, far_z * NH + far_h),
        ))
        sent[-1].start()
    result = turned[lax.div(h, 2), z]
    for number, copy in enumerate(sent):
        copy.wait_recv()
        result = result + column_in[number]
    out_ref[...] = result

    for copy in first + relay + coeff + sent:
        copy.wait_send()
    for n in range(places):
        pair(n).wait_send()
    for n in range(places - 1):
        slab(n).wait_send()


def local(right_modes, adjoint_modes, conductivity_terms):
    modes, plane = right_modes.shape[1:]
    per = conductivity_terms.shape[1]
    spaces, places = NX * NL * NC, NX * NL
    block = (4 * modes, 2 * NZ * per)
    others = 2 * NZ - 1
    return pl.pallas_call(
        assemble_kernel,
        out_shape=jax.ShapeDtypeStruct((per, 4 * modes), jnp.float32),
        in_specs=[VMEM] * 3,
        out_specs=VMEM,
        scratch_shapes=[
            pltpu.VMEM((4, 2, modes, plane), jnp.float32),
            pltpu.VMEM((2, NZ, 2, per, plane), jnp.float32),
            pltpu.VMEM((2, 8, modes, plane), jnp.float32),
            pltpu.VMEM((2, 3, modes, plane), jnp.float32),
            pltpu.VMEM((4 * NZ * per, 2 * plane), jnp.bfloat16),
            pltpu.VMEM((spaces,) + block, jnp.float32),
            pltpu.VMEM((places,) + block, jnp.float32),
            pltpu.VMEM((places,) + block, jnp.float32),
            pltpu.VMEM((max(places - 1, 1),) + block, jnp.float32),
            pltpu.VMEM((2, NZ, per, 4 * modes), jnp.float32),
            pltpu.VMEM((others, per, 4 * modes), jnp.float32),
            pltpu.SemaphoreType.DMA((6,)),
            pltpu.SemaphoreType.DMA((4, 2)),
            pltpu.SemaphoreType.DMA((2, others)),
            pltpu.SemaphoreType.DMA((2, places)),
            pltpu.SemaphoreType.DMA((2, max(places - 1, 1))),
            pltpu.SemaphoreType.DMA((2, others)),
        ],
        compiler_params=pltpu.CompilerParams(collective_id=0, has_side_effects=True),
        name="assemble_blocks",
    )(right_modes, adjoint_modes, conductivity_terms)


def solution(mesh):
    placed = (
        P(("space", "term"), None, None),
        P(("space", "term"), None, None),
        P("space", "term", None),
    )
    return jax.shard_map(
        local, mesh=mesh, in_specs=placed, out_specs=P("term", "space"), check_vma=False
    )
```

time: 315 us -> 61.5 us (0.20)
  the two profiles are of different devices: /device:TPU:16 before, /device:TPU:10 now
where the time goes in v3:
time: 61.5 us; the launch traced here: 61.3 us
  Pallas kernels  60 us (98%)
  local copies, waits for them, and re-layouts  1.3 us (2%)
    pallas_call x1, Pallas kernels, local(): pl.pallas_call(assemble_kernel, out_shape=jax.ShapeDtypeStruct((per, 4 *...  60 us
    unnamed x1, local copies, waits for them, and re-layouts  1.3 us

profile of v3, /device:TPU:10, one launch (start us, length us, event | category | flops | bytes accessed | tf_op | source)
XLA Modules:
  0.0 61.3 jit_solution(15447500255415582557)
XLA Ops:
  0.0 60.0 %assemble_blocks.1 = f32[8,256]{1,0:T(8,128)} custom-call(f32[1,64,256]{2,1,0:T(8,128)} %right_ref.1, f32[1,64,256]{2,1,0:T(8,128)} %adjoint_ref.1, f32[32,8,256]{2,1,0:T(8,128)} %coeff_ref.1), custom_call_target="tpu_custom_call" | custom-call | tf_op jit(solution)/shard_map/assemble_blocks/pallas_call | solution.py:230
  60.0 1.3 %copy.5 = f32[8,256]{1,0:T(8,128)} copy(f32[8,256]{1,0:T(8,128)} %assemble_blocks.1) | data formatting | bytes 16384

commit v4 on v3

--- a/solution.py
+++ b/solution.py
@@ -18,11 +18,11 @@
 
 def assemble_kernel(
     right_ref, adjoint_ref, coeff_ref, out_ref,
-    field, terms, flat, edges, weights, part, pair_in, mine, slab_in, turned, column_in,
-    send_sem, recv_sem, term_sem, pair_sem, slab_sem, column_sem,
+    field, terms, flat, edges, weights, part, pair_in, mine, slab_in, near_in, turned, column_in,
+    own_sem, send_sem, recv_sem, term_sem, pair_sem, slab_sem, near_sem, column_sem,
 ):
     spaces, total_terms, places = NX * NL * NC, NZ * NH, NX * NL
-    modes, plane = right_ref.shape[1:]
+    modes, plane = field.shape[2:]
     space, term = lax.axis_index("space"), lax.axis_index("term")
     c = lax.rem(space, NC)
     x, l = lax.div(space, NL * NC), lax.rem(lax.div(space, NC), NL)
@@ -41,26 +41,37 @@
         return lax.rem(z + step, NZ), (mate if other else h)
 
     def place(n):
-        return lax.rem(x + lax.rem(n + 1, NX), NX) * NL + lax.rem(l + NL - 1 - lax.div(n, NX), NL)
+        side = lax.rem(n, 2)
+        away = jnp.where(n < 2, 2, jnp.where(n < 6, 1 + 2 * side, 0))
+        across = jnp.where(n < 2, side, jnp.where(n < 4, 1 - side, jnp.where(n < 6, side, lax.rem(l + 1 + side, NL))))
+        return lax.rem(x + away, NX) * NL + across
+
+    def beside(n):
+        return (lax.rem(x + 1 + 2 * lax.rem(n, 2), NX) * NL + l) * NC + c
 
     def remote(src, dst, send, recv, target):
         return pltpu.make_async_remote_copy(
             src_ref=src, dst_ref=dst, send_sem=send, recv_sem=recv, device_id=target, device_id_type=MESH,
         )
+
+    own = 1 + odd
+    sources = (adjoint_ref.at[0], right_ref.at[0])
+    brought = [pltpu.make_async_copy(sources[kind], field.at[own, kind], own_sem.at[kind]) for kind in (0, 1)]
+    brought.append(pltpu.make_async_copy(
+        coeff_ref.at[pl.ds(z * NH + 2 * lax.div(h, 2), 2)], terms.at[lax.div(h, 2), z], own_sem.at[2]
+    ))
+    for copy in brought:
+        copy.start()
 
     barrier = pltpu.get_barrier_semaphore()
     partners = [above, below]
     for step, other in owners:
         far_z, far_h = holder(step, other)
         partners.append((space, far_z * NH + far_h))
-    partners += [(place(n) * NC + c, term) for n in range(places - 1)]
-    partners += [(place(places - 1) * NC + 1 - c, term)]
+    partners += [(beside(0), term), (beside(1), term), (place(6) * NC + c, term), (place(7) * NC + 1 - c, term)]
     for partner in partners:
         pl.semaphore_signal(barrier, inc=1, device_id=partner, device_id_type=MESH)
     pl.semaphore_wait(barrier, len(partners))
-
-    own = 1 + odd
-    sources = (adjoint_ref.at[0], right_ref.at[0])
 
     def fresh(slot, kind, number, target):
         return remote(sources[kind], field.at[slot, kind], send_sem.at[number], recv_sem.at[slot, kind], target)
@@ -96,7 +107,6 @@
 
     for copy in coeff:
         copy.start()
-    terms[lax.div(h, 2), z] = coeff_ref[pl.ds(z * NH + 2 * lax.div(h, 2), 2)]
 
     cell = lax.broadcasted_iota(jnp.int32, (modes, plane), 1)
     in_row = lax.rem(cell, GY)
@@ -107,14 +117,14 @@
             flat[kind, 4 * which + number] = values - moved(values, shift, keep)
 
     for kind in (0, 1):
-        values = sources[kind][...]
-        field[own, kind] = values
-        flatten(odd, kind, values)
+        brought[kind].wait()
+        flatten(odd, kind, field[own, kind])
 
     outer, inner, last = 3 * odd, 2 - odd, 3 - 3 * odd
     for kind in (0, 1):
         arrival(outer, kind)
         relay[kind].start()
+    brought[2].wait()
     for copy in coeff:
         copy.wait_recv()
     for slot in (0, 1):
@@ -168,9 +178,7 @@
         )
 
     def slab(n):
-        return remote(
-            mine.at[n], slab_in.at[n], slab_sem.at[0, n], slab_sem.at[1, n], (place(n) * NC + c, term)
-        )
+        return remote(mine.at[n], slab_in.at[n], slab_sem.at[0, n], slab_sem.at[1, n], (beside(n), term))
 
     def join(n):
         pair(n).wait_recv()
@@ -187,16 +195,29 @@
         @pl.when(n > 0)
         def _():
             join(n - 1)
+
+        @pl.when(jnp.logical_and(n > 4, n < 7))
+        def _():
+            slab(n - 5).wait_recv()
+            mine[n - 1] = mine[n - 1] + slab_in[n - 5]
+
+        @pl.when(jnp.logical_and(n > 0, n < 7))
+        def _():
             slab(n - 1).start()
 
         return carry
 
     lax.fori_loop(0, places, turn, 0)
+    for across in (1 - l, l):
+        slab(3 - across).wait_recv()
+        slab(4 + across).wait_recv()
+    mine[6] = mine[6] + slab_in[2 + l] + slab_in[5 - l]
+    near = remote(mine.at[6], near_in, near_sem.at[0], near_sem.at[1], (place(6) * NC + c, term))
+    near.start()
     join(places - 1)
-    total = mine[places - 1]
-    for n in range(places - 1):
-        slab(n).wait_recv()
-        total = total + slab_in[n]
+    total = mine[7] + slab_in[3 - l] + slab_in[4 + l]
+    near.wait_recv()
+    total = total + near_in[...]
     total = total.T
     turned[...] = total.reshape(turned.shape)
     sent = []
@@ -217,8 +238,9 @@
         copy.wait_send()
     for n in range(places):
         pair(n).wait_send()
-    for n in range(places - 1):
+    for n in range(6):
         slab(n).wait_send()
+    near.wait_send()
 
 
 def local(right_modes, adjoint_modes, conductivity_terms):
@@ -230,7 +252,7 @@
     return pl.pallas_call(
         assemble_kernel,
         out_shape=jax.ShapeDtypeStruct((per, 4 * modes), jnp.float32),
-        in_specs=[VMEM] * 3,
+        in_specs=[pl.BlockSpec(memory_space=pl.ANY)] * 3,
         out_specs=VMEM,
         scratch_shapes=[
             pltpu.VMEM((4, 2, modes, plane), jnp.float32),
@@ -241,14 +263,17 @@
             pltpu.VMEM((spaces,) + block, jnp.float32),
             pltpu.VMEM((places,) + block, jnp.float32),
             pltpu.VMEM((places,) + block, jnp.float32),
-            pltpu.VMEM((max(places - 1, 1),) + block, jnp.float32),
+            pltpu.VMEM((6,) + block, jnp.float32),
+            pltpu.VMEM(block, jnp.float32),
             pltpu.VMEM((2, NZ, per, 4 * modes), jnp.float32),
             pltpu.VMEM((others, per, 4 * modes), jnp.float32),
+            pltpu.SemaphoreType.DMA((3,)),
             pltpu.SemaphoreType.DMA((6,)),
             pltpu.SemaphoreType.DMA((4, 2)),
             pltpu.SemaphoreType.DMA((2, others)),
             pltpu.SemaphoreType.DMA((2, places)),
-            pltpu.SemaphoreType.DMA((2, max(places - 1, 1))),
+            pltpu.SemaphoreType.DMA((2, 6)),
+            pltpu.SemaphoreType.DMA((2,)),
             pltpu.SemaphoreType.DMA((2, others)),
         ],
         compiler_params=pltpu.CompilerParams(collective_id=0, has_side_effects=True),

time: 61.5 us -> 59.2 us (0.963)
  the two profiles are of different devices: /device:TPU:10 before, /device:TPU:8 now
where the time goes in v4:
time: 59.2 us; the launch traced here: 59 us
  Pallas kernels  57.7 us (97%)
  local copies, waits for them, and re-layouts  1.3 us (2%)
    pallas_call x1, Pallas kernels, local(): pl.pallas_call(assemble_kernel, out_shape=jax.ShapeDtypeStruct((per, 4 *...  57.7 us
    unnamed x1, local copies, waits for them, and re-layouts  1.3 us

profile of v4, /device:TPU:8, one launch (start us, length us, event | category | flops | bytes accessed | tf_op | source)
XLA Modules:
  0.0 59.0 jit_solution(4004107333313388419)
XLA Ops:
  0.0 57.7 %assemble_blocks.1 = f32[8,256]{1,0:T(8,128)} custom-call(f32[1,64,256]{2,1,0:T(8,128)} %right_ref.1, f32[1,64,256]{2,1,0:T(8,128)} %adjoint_ref.1, f32[32,8,256]{2,1,0:T(8,128)} %coeff_ref.1), custom_call_target="tpu_custom_call" | custom-call | tf_op jit(solution)/shard_map/assemble_blocks/pallas_call | solution.py:252
  57.7 1.3 %copy.5 = f32[8,256]{1,0:T(8,128)} copy(f32[8,256]{1,0:T(8,128)} %assemble_blocks.1) | data formatting | bytes 16384

commit v5 on v4

--- a/solution.py
+++ b/solution.py
@@ -18,8 +18,9 @@
 
 def assemble_kernel(
     right_ref, adjoint_ref, coeff_ref, out_ref,
-    field, terms, flat, edges, weights, part, pair_in, mine, slab_in, near_in, turned, column_in,
-    own_sem, send_sem, recv_sem, term_sem, pair_sem, slab_sem, near_sem, column_sem,
+    field, terms, flat, edges, inside, weights, part, pair_in, mine, slab_in, near_in, across_in, half_in, side_in,
+    turned, column_in,
+    own_sem, send_sem, recv_sem, term_sem, pair_sem, slab_sem, near_sem, across_sem, half_sem, side_sem, column_sem,
 ):
     spaces, total_terms, places = NX * NL * NC, NZ * NH, NX * NL
     modes, plane = field.shape[2:]
@@ -43,8 +44,8 @@
     def place(n):
         side = lax.rem(n, 2)
         away = jnp.where(n < 2, 2, jnp.where(n < 6, 1 + 2 * side, 0))
-        across = jnp.where(n < 2, side, jnp.where(n < 4, 1 - side, jnp.where(n < 6, side, lax.rem(l + 1 + side, NL))))
-        return lax.rem(x + away, NX) * NL + across
+        here = jnp.where(n < 2, side, jnp.where(n < 4, 1 - side, side))
+        return lax.rem(x + away, NX) * NL + lax.rem(l + 1 + here, NL)
 
     def beside(n):
         return (lax.rem(x + 1 + 2 * lax.rem(n, 2), NX) * NL + l) * NC + c
@@ -79,8 +80,9 @@
     def arrival(slot, kind):
         pltpu.make_async_copy(field.at[slot, kind], field.at[slot, kind], recv_sem.at[slot, kind]).wait()
 
-    first = [fresh(1 - odd, kind, kind, above) for kind in (0, 1)]
-    first += [fresh(3 - odd, kind, 2 + kind, below) for kind in (0, 1)]
+    outward = tuple(jnp.where(odd == 1, up, down) for up, down in zip(above, below))
+    to_outer = [fresh(3 - 3 * odd, kind, kind, outward) for kind in (0, 1)]
+    to_inner = [fresh(own, kind, 2 + kind, partner_of_pair) for kind in (0, 1)]
     relay = [
         remote(
             field.at[3 * odd, kind], field.at[3 * odd, kind], send_sem.at[4 + kind], recv_sem.at[3 * odd, kind],
@@ -95,18 +97,11 @@
             coeff_ref.at[pl.ds(far_z * NH + 2 * lax.div(far_h, 2), 2)], terms.at[lax.div(h, 2), z],
             term_sem.at[0, number], term_sem.at[1, number], (space, far_z * NH + far_h),
         ))
-    @pl.when(odd == 0)
-    def _():
-        for copy in (first[2], first[3], first[0], first[1]):
+    to_outer[0].start()
+    to_inner[0].start()
+    for (step, other), copy in zip(owners, coeff):
+        if not other:
             copy.start()
-
-    @pl.when(odd == 1)
-    def _():
-        for copy in first:
-            copy.start()
-
-    for copy in coeff:
-        copy.start()
 
     cell = lax.broadcasted_iota(jnp.int32, (modes, plane), 1)
     in_row = lax.rem(cell, GY)
@@ -116,14 +111,38 @@
         for number, (shift, keep) in enumerate(keeps):
             flat[kind, 4 * which + number] = values - moved(values, shift, keep)
 
+    def fill(which):
+        def step(row, carry):
+            value = None
+            for number in range(4):
+                product = flat[0, 4 * which + number, pl.ds(row, 1), :] * flat[1, 4 * which + number]
+                value = product if value is None else value + product
+            inside[which, row] = value
+            return carry
+
+        lax.fori_loop(0, modes, step, 0, unroll=4)
+
     for kind in (0, 1):
         brought[kind].wait()
         flatten(odd, kind, field[own, kind])
+    fill(odd)
 
     outer, inner, last = 3 * odd, 2 - odd, 3 - 3 * odd
+    for copies in (to_outer, to_inner):
+        copies[0].wait_send()
+        copies[1].start()
+    arrival(outer, 0)
+    relay[0].start()
+    to_outer[1].wait_send()
+    for (step, other), copy in zip(owners, coeff):
+        if other:
+            copy.start()
+    arrival(outer, 1)
+    relay[1].start()
     for kind in (0, 1):
-        arrival(outer, kind)
-        relay[kind].start()
+        arrival(inner, kind)
+        flatten(1 - odd, kind, field[inner, kind])
+    fill(1 - odd)
     brought[2].wait()
     for copy in coeff:
         copy.wait_recv()
@@ -133,9 +152,6 @@
         lower = (value - upper.astype(jnp.float32)).astype(jnp.bfloat16)
         weights[:, slot * plane:(slot + 1) * plane] = jnp.concatenate([upper, lower], axis=0)
     for kind in (0, 1):
-        arrival(inner, kind)
-        flatten(1 - odd, kind, field[inner, kind])
-    for kind in (0, 1):
         arrival(last, kind)
 
     lowest = jnp.logical_and(space == 0, term < 2)
@@ -156,10 +172,7 @@
             borders = [edges[0, slot, pl.ds(row, 1), :] * edges[1, slot] for slot in range(3)]
             values = []
             for slot in (0, 1):
-                value = borders[slot] + borders[slot + 1]
-                for number in range(4 * slot, 4 * slot + 4):
-                    value = value + flat[0, number, pl.ds(row, 1), :] * flat[1, number]
-                values.append(value)
+                values.append(borders[slot] + borders[slot + 1] + inside[slot, row])
             value = jnp.concatenate(values, axis=1)
             upper = value.astype(jnp.bfloat16)
             left += [upper, (value - upper.astype(jnp.float32)).astype(jnp.bfloat16)]
@@ -177,12 +190,41 @@
             (place(places - 1) * NC + 1 - c, term),
         )
 
+    half = mine.shape[1] // 2
+    quarter = half // 2
+    first, second = pl.ds(0, half), pl.ds(half, half)
+    beyond = (place(6) * NC + c, term)
+
     def slab(n):
-        return remote(mine.at[n], slab_in.at[n], slab_sem.at[0, n], slab_sem.at[1, n], (beside(n), term))
+        return remote(mine.at[n, first], slab_in.at[n], slab_sem.at[0, n], slab_sem.at[1, n], (beside(n), term))
+
+    crossing = (0, 3, 4, 6)
+
+    def cross(number):
+        return remote(
+            mine.at[crossing[number], second], across_in.at[number], across_sem.at[0, number],
+            across_sem.at[1, number], beyond,
+        )
+
+    def part_way(side):
+        return remote(
+            mine.at[1, pl.ds(half + side * quarter, quarter)], half_in.at[side], half_sem.at[0, side],
+            half_sem.at[1, side], (beside(side), term),
+        )
+
+    def sideways(side):
+        return remote(
+            mine.at[2 + 3 * side, second], side_in.at[side], side_sem.at[0, side], side_sem.at[1, side],
+            (beside(side), term),
+        )
 
     def join(n):
         pair(n).wait_recv()
         mine[n] = part[place(n) * NC + c] + pair_in[n]
+        if n < 4:
+            slab(n).start()
+        if n in crossing:
+            cross(crossing.index(n)).start()
 
     def turn(n, carry):
         def step(k, carry):
@@ -191,33 +233,45 @@
 
         lax.fori_loop(0, 2, step, 0)
         pair(n).start()
-
-        @pl.when(n > 0)
-        def _():
-            join(n - 1)
-
-        @pl.when(jnp.logical_and(n > 4, n < 7))
-        def _():
-            slab(n - 5).wait_recv()
-            mine[n - 1] = mine[n - 1] + slab_in[n - 5]
-
-        @pl.when(jnp.logical_and(n > 0, n < 7))
-        def _():
-            slab(n - 1).start()
+        for done in range(places - 1):
+            @pl.when(n == done + 1)
+            def _(done=done):
+                join(done)
 
         return carry
 
     lax.fori_loop(0, places, turn, 0)
-    for across in (1 - l, l):
-        slab(3 - across).wait_recv()
-        slab(4 + across).wait_recv()
-    mine[6] = mine[6] + slab_in[2 + l] + slab_in[5 - l]
-    near = remote(mine.at[6], near_in, near_sem.at[0], near_sem.at[1], (place(6) * NC + c, term))
+    for side in (0, 1):
+        slab(side).wait_recv()
+        mine[4 + side, first] = mine[4 + side, first] + slab_in[side]
+        slab(4 + side).start()
+    cross(0).wait_recv()
+    mine[1, second] = mine[1, second] + across_in[0]
+    for side in (0, 1):
+        part_way(side).start()
+    join(places - 1)
+    for side in (1, 0):
+        cross(2 - side).wait_recv()
+        mine[2 + 3 * side, second] = mine[2 + 3 * side, second] + across_in[2 - side]
+        part_way(side).wait_recv()
+        rows = pl.ds(half + side * quarter, quarter)
+        mine[2 + 3 * side, rows] = mine[2 + 3 * side, rows] + half_in[side]
+        sideways(side).start()
+    slab(3).wait_recv()
+    slab(4).wait_recv()
+    mine[6, first] = mine[6, first] + slab_in[3] + slab_in[4]
+    near = remote(mine.at[6, first], near_in, near_sem.at[0], near_sem.at[1], beyond)
     near.start()
-    join(places - 1)
-    total = mine[7] + slab_in[3 - l] + slab_in[4 + l]
+    slab(2).wait_recv()
+    slab(5).wait_recv()
+    upper = mine[7, first] + slab_in[2] + slab_in[5]
+    cross(3).wait_recv()
+    lower = mine[7, second] + across_in[3]
+    for side in (0, 1):
+        sideways(side).wait_recv()
+        lower = lower + side_in[side]
     near.wait_recv()
-    total = total + near_in[...]
+    total = jnp.concatenate([upper + near_in[...], lower], axis=0)
     total = total.T
     turned[...] = total.reshape(turned.shape)
     sent = []
@@ -234,13 +288,18 @@
         result = result + column_in[number]
     out_ref[...] = result
 
-    for copy in first + relay + coeff + sent:
+    for copy in to_inner[1:] + relay + coeff + sent:
         copy.wait_send()
     for n in range(places):
         pair(n).wait_send()
     for n in range(6):
         slab(n).wait_send()
     near.wait_send()
+    for number in range(len(crossing)):
+        cross(number).wait_send()
+    for side in (0, 1):
+        part_way(side).wait_send()
+        sideways(side).wait_send()
 
 
 def local(right_modes, adjoint_modes, conductivity_terms):
@@ -259,12 +318,16 @@
             pltpu.VMEM((2, NZ, 2, per, plane), jnp.float32),
             pltpu.VMEM((2, 8, modes, plane), jnp.float32),
             pltpu.VMEM((2, 3, modes, plane), jnp.float32),
+            pltpu.VMEM((2, modes, modes, plane), jnp.float32),
             pltpu.VMEM((4 * NZ * per, 2 * plane), jnp.bfloat16),
             pltpu.VMEM((spaces,) + block, jnp.float32),
             pltpu.VMEM((places,) + block, jnp.float32),
             pltpu.VMEM((places,) + block, jnp.float32),
-            pltpu.VMEM((6,) + block, jnp.float32),
-            pltpu.VMEM(block, jnp.float32),
+            pltpu.VMEM((6, 2 * modes, block[1]), jnp.float32),
+            pltpu.VMEM((2 * modes, block[1]), jnp.float32),
+            pltpu.VMEM((4, 2 * modes, block[1]), jnp.float32),
+            pltpu.VMEM((2, modes, block[1]), jnp.float32),
+            pltpu.VMEM((2, 2 * modes, block[1]), jnp.float32),
             pltpu.VMEM((2, NZ, per, 4 * modes), jnp.float32),
             pltpu.VMEM((others, per, 4 * modes), jnp.float32),
             pltpu.SemaphoreType.DMA((3,)),
@@ -274,6 +337,9 @@
             pltpu.SemaphoreType.DMA((2, places)),
             pltpu.SemaphoreType.DMA((2, 6)),
             pltpu.SemaphoreType.DMA((2,)),
+            pltpu.SemaphoreType.DMA((2, 4)),
+            pltpu.SemaphoreType.DMA((2, 2)),
+            pltpu.SemaphoreType.DMA((2, 2)),
             pltpu.SemaphoreType.DMA((2, others)),
         ],
         compiler_params=pltpu.CompilerParams(collective_id=0, has_side_effects=True),

time: 59.2 us -> 56.2 us (0.949)
  Pallas kernels: 57.7 us -> 54.7 us
    pallas_call x1, Pallas kernels: 57.7 us -> 54.7 us  [local(): pl.pallas_call(assemble_kernel, out_shape=jax.ShapeDtypeStruct((per, 4 *...]
where the time goes in v5:
time: 56.2 us; the launch traced here: 56 us
  Pallas kernels  54.7 us (97%)
  local copies, waits for them, and re-layouts  1.3 us (2%)
    pallas_call x1, Pallas kernels, local(): pl.pallas_call(assemble_kernel, out_shape=jax.ShapeDtypeStruct((per, 4 *...  54.7 us
    unnamed x1, local copies, waits for them, and re-layouts  1.3 us

profile of v5, /device:TPU:8, one launch (start us, length us, event | category | flops | bytes accessed | tf_op | source)
XLA Modules:
  0.0 56.0 jit_solution(12794061172673169490)
XLA Ops:
  0.0 54.7 %assemble_blocks.1 = f32[8,256]{1,0:T(8,128)} custom-call(f32[1,64,256]{2,1,0:T(8,128)} %right_ref.1, f32[1,64,256]{2,1,0:T(8,128)} %adjoint_ref.1, f32[32,8,256]{2,1,0:T(8,128)} %coeff_ref.1), custom_call_target="tpu_custom_call" | custom-call | tf_op jit(solution)/shard_map/assemble_blocks/pallas_call | solution.py:311
  54.7 1.3 %copy.5 = f32[8,256]{1,0:T(8,128)} copy(f32[8,256]{1,0:T(8,128)} %assemble_blocks.1) | data formatting | bytes 16384

commit v6 on v5

--- a/solution.py
+++ b/solution.py
@@ -36,7 +36,8 @@
 
     above, below = owner(lax.rem(index + 1, planes)), owner(lax.rem(index + planes - 1, planes))
     partner_of_pair = owner(index + 1 - 2 * odd)
-    owners = [(step, other) for step in range(NZ) for other in (0, 1)][1:]
+    steps = sorted(range(NZ), key=lambda step: abs(2 * step - NZ))
+    owners = [(step, other) for step in steps for other in (0, 1) if step or other]
 
     def holder(step, other):
         return lax.rem(z + step, NZ), (mate if other else h)
@@ -97,11 +98,12 @@
             coeff_ref.at[pl.ds(far_z * NH + 2 * lax.div(far_h, 2), 2)], terms.at[lax.div(h, 2), z],
             term_sem.at[0, number], term_sem.at[1, number], (space, far_z * NH + far_h),
         ))
-    to_outer[0].start()
-    to_inner[0].start()
-    for (step, other), copy in zip(owners, coeff):
-        if not other:
-            copy.start()
+    for copy in to_outer + to_inner:
+        copy.start()
+    for crossed in (0, 1):
+        for (step, other), copy in zip(owners, coeff):
+            if other == crossed:
+                copy.start()
 
     cell = lax.broadcasted_iota(jnp.int32, (modes, plane), 1)
     in_row = lax.rem(cell, GY)
@@ -128,17 +130,9 @@
     fill(odd)
 
     outer, inner, last = 3 * odd, 2 - odd, 3 - 3 * odd
-    for copies in (to_outer, to_inner):
-        copies[0].wait_send()
-        copies[1].start()
-    arrival(outer, 0)
-    relay[0].start()
-    to_outer[1].wait_send()
-    for (step, other), copy in zip(owners, coeff):
-        if other:
-            copy.start()
-    arrival(outer, 1)
-    relay[1].start()
+    for kind in (0, 1):
+        arrival(outer, kind)
+        relay[kind].start()
     for kind in (0, 1):
         arrival(inner, kind)
         flatten(1 - odd, kind, field[inner, kind])
@@ -165,10 +159,9 @@
 
     count = weights.shape[0] // 2
 
-    def assemble(d):
+    def assemble(blocks):
         left = []
-        for row in range(4):
-            row = 4 * d + row
+        for row in [4 * d + row for d in blocks for row in range(4)]:
             borders = [edges[0, slot, pl.ds(row, 1), :] * edges[1, slot] for slot in range(3)]
             values = []
             for slot in (0, 1):
@@ -180,9 +173,10 @@
             jnp.concatenate(left, axis=0), weights[...], (((1,), (1,)), ((), ())), preferred_element_type=jnp.float32,
         )
         total = total[:, :count] + total[:, count:]
-        for row in range(4):
-            at = 2 * row * modes
-            part[d, row * modes:(row + 1) * modes, :] = total[at:at + modes] + total[at + modes:at + 2 * modes]
+        for number, d in enumerate(blocks):
+            for row in range(4):
+                at = 2 * (4 * number + row) * modes
+                part[d, row * modes:(row + 1) * modes, :] = total[at:at + modes] + total[at + modes:at + 2 * modes]
 
     def pair(n):
         return remote(
@@ -227,28 +221,26 @@
             cross(crossing.index(n)).start()
 
     def turn(n, carry):
-        def step(k, carry):
-            assemble(place(n) * NC + lax.rem(c + 1 + k, 2))
-            return carry
-
-        lax.fori_loop(0, 2, step, 0)
+        assemble([place(n) * NC + 1 - c, place(n) * NC + c])
         pair(n).start()
         for done in range(places - 1):
             @pl.when(n == done + 1)
             def _(done=done):
                 join(done)
+                if done in (4, 5):
+                    side = done - 4
+                    slab(side).wait_recv()
+                    mine[done, first] = mine[done, first] + slab_in[side]
+                    slab(done).start()
+                if done == 5:
+                    cross(0).wait_recv()
+                    mine[1, second] = mine[1, second] + across_in[0]
+                    for side in (0, 1):
+                        part_way(side).start()
 
         return carry
 
     lax.fori_loop(0, places, turn, 0)
-    for side in (0, 1):
-        slab(side).wait_recv()
-        mine[4 + side, first] = mine[4 + side, first] + slab_in[side]
-        slab(4 + side).start()
-    cross(0).wait_recv()
-    mine[1, second] = mine[1, second] + across_in[0]
-    for side in (0, 1):
-        part_way(side).start()
     join(places - 1)
     for side in (1, 0):
         cross(2 - side).wait_recv()
@@ -288,7 +280,7 @@
         result = result + column_in[number]
     out_ref[...] = result
 
-    for copy in to_inner[1:] + relay + coeff + sent:
+    for copy in to_outer + to_inner + relay + coeff + sent:
         copy.wait_send()
     for n in range(places):
         pair(n).wait_send()

time: 56.2 us -> 55.3 us (0.984)
  Pallas kernels: 54.7 us -> 53.8 us
    pallas_call x1, Pallas kernels: 54.7 us -> 53.8 us  [local(): pl.pallas_call(assemble_kernel, out_shape=jax.ShapeDtypeStruct((per, 4 *...]
where the time goes in v6:
time: 55.3 us; the launch traced here: 55.1 us
  Pallas kernels  53.8 us (97%)
  local copies, waits for them, and re-layouts  1.3 us (2%)
    pallas_call x1, Pallas kernels, local(): pl.pallas_call(assemble_kernel, out_shape=jax.ShapeDtypeStruct((per, 4 *...  53.8 us
    unnamed x1, local copies, waits for them, and re-layouts  1.3 us

profile of v6, /device:TPU:8, one launch (start us, length us, event | category | flops | bytes accessed | tf_op | source)
XLA Modules:
  0.0 55.1 jit_solution(10452077471813787035)
XLA Ops:
  0.0 53.8 %assemble_blocks.1 = f32[8,256]{1,0:T(8,128)} custom-call(f32[1,64,256]{2,1,0:T(8,128)} %right_ref.1, f32[1,64,256]{2,1,0:T(8,128)} %adjoint_ref.1, f32[32,8,256]{2,1,0:T(8,128)} %coeff_ref.1), custom_call_target="tpu_custom_call" | custom-call | tf_op jit(solution)/shard_map/assemble_blocks/pallas_call | solution.py:303
  53.8 1.3 %copy.5 = f32[8,256]{1,0:T(8,128)} copy(f32[8,256]{1,0:T(8,128)} %assemble_blocks.1) | data formatting | bytes 16384
